TPU v7x, 32 devices: a whole 2x2x4 slice. The times are simulated.
32 devices in a mesh: blk: 16 (over z, y, core), uly: 2 (over x).
Axes of the slice: x: 2, y: 2, z: 4, core: 2. Of those that a mesh axis runs over, the one named last changes fastest.
Arguments:
- queries: bfloat16 [8192, 6144], P(('blk', 'uly')), may hold values from -8 to 8
- keys: bfloat16 [2048, 6144], P(('blk', 'uly')), may hold values from -8 to 8
- values: bfloat16 [2048, 6144], P(('blk', 'uly')), may hold values from -6 to 6
- block_lists: int32 [48, 64, 16], replicated, may hold values from 0 to 15, as said below
- block_counts: int32 [48, 64], replicated, may hold values from 1 to 16, as said below
Outputs:
- attended: bfloat16 [8192, 6144], P(('blk', 'uly'))
Inputs may be any that keep to these rules, and one draw needn't show every extreme that they name: `block_lists`: entry 0 of the list for query block a is always the key block at the same relative place in the sequence, the integer part of a times 16 divided by 64; the first block_counts entries of a list are distinct key blocks; entries after them are key block numbers that are ignored. `block_counts`: counts differ widely from head to head.
All inputs are finite; a program needn't handle non-finite values.
Results may differ from a plain program's by a relative error of at most 0.0055.
Values may be sent and summed in bfloat16 or wider, within the bound.
A program may use at most 256 MiB of HBM per device.

v0:
```python
import math

import jax
import jax.numpy as jnp
from jax import lax
from jax.sharding import PartitionSpec as P

HEADS = 48
HEAD_DIM = 128
BLOCK = 128


NEGATIVE = -1e30


def tile_update(state, query_heads, key_heads, value_heads, allowed, scaling):
    totals, maxima, sums = state
    scores = (
        jnp.einsum("qhd,khd->hqk", query_heads, key_heads, preferred_element_type=jnp.float32)
        * scaling
    )
    highest = jnp.maximum(maxima, jnp.max(jnp.where(allowed, scores, NEGATIVE), axis=2))
    weights = jnp.where(allowed, jnp.exp(scores - highest[:, :, None]), 0.0)
    sums = jnp.sum(weights, axis=2)
    mixed = jnp.einsum(
        "hqk,khd->hqd",
        weights.astype(jnp.bfloat16),
        value_heads,
        preferred_element_type=jnp.float32,
    )
    totals = mixed
    return (totals, highest, sums)


def local(queries, keys, values, block_lists, block_counts):
    uly_count = lax.axis_size("uly")
    blk_count = lax.axis_size("blk")
    uly_index = lax.axis_index("uly")
    blk_index = lax.axis_index("blk")
    per_device = HEADS // uly_count
    scaling = 1.0 / math.sqrt(HEAD_DIM)
    head_numbers = jnp.arange(HEADS, dtype=jnp.int32)
    query_local, key_local, value_local = (queries, keys, values)
    query_mine, key_mine, value_mine = (
        lax.all_to_all(query_local, "uly", split_axis=1, concat_axis=0, tiled=True),
        lax.all_to_all(key_local, "uly", split_axis=1, concat_axis=0, tiled=True),
        lax.all_to_all(value_local, "uly", split_axis=1, concat_axis=0, tiled=True),
    )
    query_rows = query_mine.shape[0]
    key_rows = key_mine.shape[0]
    query_blocks_here = query_rows // BLOCK
    key_blocks_all = key_rows * blk_count // BLOCK
    query_heads = query_mine.reshape(query_rows, per_device, HEAD_DIM)
    heads_here = lax.dynamic_slice_in_dim(head_numbers, uly_index * per_device, per_device)
    lists_here = lax.dynamic_slice_in_dim(
        jnp.take(block_lists, heads_here, axis=0),
        blk_index * query_blocks_here,
        query_blocks_here,
        1,
    )
    counts_here = lax.dynamic_slice_in_dim(
        jnp.take(block_counts, heads_here, axis=0),
        blk_index * query_blocks_here,
        query_blocks_here,
        1,
    )
    usable = (
        jnp.arange(lists_here.shape[2], dtype=jnp.int32)[None, None, :] < counts_here[:, :, None]
    )
    matches = (
        lists_here[:, :, :, None]
        == jnp.arange(key_blocks_all, dtype=jnp.int32)[None, None, None, :]
    ) & usable[:, :, :, None]
    member = jnp.any(matches, axis=2)
    initial = (
        jnp.zeros((per_device, query_rows, HEAD_DIM), jnp.float32),
        jnp.full((per_device, query_rows), NEGATIVE, jnp.float32),
        jnp.zeros((per_device, query_rows), jnp.float32),
    )
    key_piece = lax.all_gather(key_mine, "blk", axis=0, tiled=True)
    row_count = key_piece.shape[0]
    key_heads = key_piece.reshape(row_count, per_device, HEAD_DIM)
    value_heads = lax.all_gather(value_mine, "blk", axis=0, tiled=True).reshape(
        row_count, per_device, HEAD_DIM
    )
    block_number = jnp.arange(row_count, dtype=jnp.int32) // BLOCK
    member_cols = jnp.take(member, block_number, axis=2)
    allowed = jnp.broadcast_to(
        member_cols[:, :, None, :], (per_device, query_blocks_here, BLOCK, row_count)
    )
    allowed = allowed.reshape(per_device, query_rows, row_count)
    final = tile_update(initial, query_heads, key_heads, value_heads, allowed, scaling)
    totals, maxima, sums = final
    normalized = (totals / sums[:, :, None]).astype(jnp.bfloat16)
    outgoing = jnp.transpose(normalized, (1, 0, 2)).reshape(query_rows, per_device * HEAD_DIM)
    returned = lax.all_to_all(outgoing, "uly", split_axis=0, concat_axis=1, tiled=True)
    return returned


def solution(mesh):
    return jax.shard_map(
        local,
        mesh=mesh,
        in_specs=(
            P(("blk", "uly"), None),
            P(("blk", "uly"), None),
            P(("blk", "uly"), None),
            P(),
            P(),
        ),
        out_specs=P(("blk", "uly"), None),
        check_vma=False,
    )
```

profile of v0, /device:TPU:0, one launch (start us, length us, event | category | flops | bytes accessed | tf_op | source)
XLA Modules:
  0.0 337.3 jit_solution(4696372482445700008)
XLA Ops:
  6.5 1.2 copy.72
  7.8 15.5 %all_to_all.73 = bf16[64,2,3072]{2,0,1:T(8,128)(2,1)} all-to-all(bf16[64,2,3072]{2,0,1:T(8,128)(2,1)S(1)} %bitcast.56), channel_id=1, replica_groups=mesh['blk'=16,'uly'=2] {'uly'}, dimensions={1} | all-to-all | bytes 1572864 | tf_op jit(solution)/shard_map/all_to_all | solution.py:46
  23.3 1.2 copy.71
  24.5 13.7 %all_to_all.74 = bf16[64,2,3072]{2,0,1:T(8,128)(2,1)} all-to-all(bf16[64,2,3072]{2,0,1:T(8,128)(2,1)S(1)} %bitcast.57), channel_id=1, replica_groups=mesh['blk'=16,'uly'=2] {'uly'}, dimensions={1} | all-to-all | bytes 1572864 | tf_op jit(solution)/shard_map/all_to_all | solution.py:47
  38.2 3.8 %copy.70 = bf16[32,2,8,3072]{3,2,0,1:T(8,128)(2,1)} copy(bf16[32,2,8,3072]{3,2,1,0:T(8,128)(2,1)} %bitcast.53) | data formatting | bytes 6291456 | tf_op jit(solution)/shard_map/all_to_all | solution.py:45
  42.0 4.0 %all-to-all-start = ((bf16[256,2,3072]{2,0,1:T(8,128)(2,1)}), bf16[256,2,3072]{2,0,1:T(8,128)(2,1)S(1)}, u32[]{:S(2)}, u32[]{:S(2)}) async-start(bf16[256,2,3072]{2,0,1:T(8,128)(2,1)} %bitcast.49), calls=%async_computation | async-start | bytes 6291456 | tf_op jit(solution)/shard_map/all_to_all | solution.py:45
  46.1 1.3 gather_fusion
  47.3 1.3 gather_fusion.1
  50.3 13.8 %gather_fusion.2 = pred[2048,24,4]{1,2,0:T(4,128)(4,1)} fusion(pred[24,4,16]{0,1,2:T(4,128)(4,1)S(1)} %copy.44, s32[2048]{0:T(1024)S(1)} %broadcast_clamp_fusion), kind=kCustom, calls=%fused_computation.2 | custom fusion | bytes 401408 | tf_op jit(solution)/shard_map/jit(_take)/gather | solution.py:87
  64.0 10.6 %select_bitcast_fusion = pred[24,4,2048]{0,1,2:T(4,128)(4,1)} fusion(pred[2048,24,4]{1,2,0:T(4,128)(4,1)} %gather_fusion.2, pred[2048]{0:T(1024)(128)(4,1)S(1)} %fusion.12), kind=kLoop, calls=%fused_computation.10 | loop fusion | flops 196608 | bytes 395264 | tf_op jit(solution)/shard_map/jit(_take)/select_n | solution.py:87
  74.6 3.1 copy.45
  77.7 3.2 all-to-all-done
  80.9 2.5 copy.62
  83.4 41.0 %all-gather.3.cloned.1.call-done = bf16[2048,3072]{1,0:T(8,128)(2,1)} async-done(((bf16[128,3072]{1,0:T(8,128)(2,1)}), bf16[2048,3072]{1,0:T(8,128)(2,1)}) %all-gather.3.cloned.1.call-update) | async-done | bytes 12582928 | tf_op jit(solution)/shard_map/all_gather | solution.py:80
  124.4 16.8 %copy.48 = bf16[2048,3072]{0,1:T(8,128)(2,1)} copy(bf16[2048,3072]{1,0:T(8,128)(2,1)} %all-gather.3.cloned.1.call-done) | data formatting | bytes 25165824 | tf_op jit(solution)/shard_map/all_gather | solution.py:80
  141.2 42.1 %fusion = (f32[24,512]{1,0:T(8,128)S(1)}, f32[24,512,2048]{2,1,0:T(8,128)}) fusion(pred[24,4,2048]{2,1,0:T(4,128)(4,1)S(1)} %copy.45, bf16[2048,24,128]{0,2,1:T(8,128)(2,1)} %bitcast.46, bf16[512,24,128]{2,1,0:T(8,128)(2,1)S(1)} %bitcast.52), kind=kOutput, calls=%fused_computation.5 | convolution fusion | flops 6517936128 | bytes 116637696 | tf_op jit(solution)/shard_map/qhd,khd->hqk/dot_general | solution.py:19
  183.3 50.0 %fusion.2 = (bf16[24,512,2048]{2,1,0:T(8,128)(2,1)}, f32[24,512]{1,0:T(8,128)S(1)}) fusion(f32[24,512,2048]{2,1,0:T(8,128)} %get-tuple-element.10, f32[24,512]{1,0:T(8,128)S(1)} %broadcast_maximum_fusion, pred[24,4,2048]{2,1,0:T(4,128)(4,1)S(1)} %copy.45), kind=kLoop, calls=%fused_computation.7 | loop fusion | flops 125816832 | bytes 151289856 | tf_op jit(solution)/shard_map/convert_element_type | solution.py:27
  233.3 16.6 %copy.52 = bf16[2048,3072]{0,1:T(8,128)(2,1)} copy(bf16[2048,3072]{1,0:T(8,128)(2,1)} %all-gather.5.cloned.1.call-done) | data formatting | bytes 25165824 | tf_op jit(solution)/shard_map/all_gather | solution.py:83
  250.0 25.3 %fusion.3 = bf16[512,24,128]{2,0,1:T(8,128)(2,1)} fusion(f32[512,24]{0,1:T(8,128)S(1)} %bitcast.60, bf16[24,512,2048]{2,1,0:T(8,128)(2,1)} %get-tuple-element.7, bf16[2048,24,128]{0,2,1:T(8,128)(2,1)} %bitcast.47), kind=kOutput, calls=%fused_computation.9 | convolution fusion | flops 6445596672 | bytes 66109440 | tf_op jit(solution)/shard_map/hqk,khd->hqd/dot_general | solution.py:25
  275.3 4.0 %copy.54 = bf16[512,24,128]{2,1,0:T(8,128)(2,1)S(1)} copy(bf16[512,24,128]{2,0,1:T(8,128)(2,1)} %fusion.3) | data formatting | bytes 6291456 | tf_op jit(solution)/shard_map/convert_element_type | solution.py:94
  279.3 2.8 all_to_all.65
  282.1 41.0 %all_to_all.75 = bf16[2,256,3072]{2,1,0:T(8,128)(2,1)S(1)} all-to-all(bf16[2,256,3072]{2,1,0:T(8,128)(2,1)} %all_to_all.65), channel_id=1, replica_groups=mesh['blk'=16,'uly'=2] {'uly'}, dimensions={0} | all-to-all | bytes 6291456 | tf_op jit(solution)/shard_map/all_to_all | solution.py:96
  323.0 2.8 copy.55
  325.8 4.6 %copy.56 = bf16[256,6144]{1,0:T(8,128)(2,1)} copy(bf16[256,6144]{0,1:T(8,128)(2,1)} %bitcast.51) | data formatting | bytes 6291456 | tf_op jit(solution)/shard_map/all_to_all | solution.py:96
  (25 shorter events, 1.8 us)
Async XLA Ops:
  6.5 39.5 %copy-start = (s32[48,64,16]{1,2,0:T(8,128)S(1)}, s32[48,64,16]{1,2,0:T(8,128)}, u32[]{:S(2)}) copy-start(s32[48,64,16]{1,2,0:T(8,128)} %param.8) | copy-start | bytes 589828
  6.5 117.9 %all-gather.3.cloned.1.call-start = ((), (), s32[]{:S(2)}) async-start(), calls=%async_computation.4 | async-start | bytes 13369344 | tf_op jit(solution)/shard_map/all_gather | solution.py:80
  23.3 210.1 %all-gather.5.cloned.1.call-start = ((), (), s32[]{:S(2)}) async-start(), calls=%async_computation.5 | async-start | bytes 13369344 | tf_op jit(solution)/shard_map/all_gather | solution.py:83
  42.0 38.9 %all-to-all-start = ((bf16[256,2,3072]{2,0,1:T(8,128)(2,1)}), bf16[256,2,3072]{2,0,1:T(8,128)(2,1)S(1)}, u32[]{:S(2)}, u32[]{:S(2)}) async-start(bf16[256,2,3072]{2,0,1:T(8,128)(2,1)} %bitcast.49), calls=%async_computation | async-start | bytes 6291456 | tf_op jit(solution)/shard_map/all_to_all | solution.py:45
  83.4 57.8 %copy-start.2 = (bf16[64,8,24,128]{3,2,1,0:T(8,128)(2,1)S(1)}, bf16[64,8,24,128]{3,2,1,0:T(8,128)(2,1)}, u32[]{:S(2)}) copy-start(bf16[64,8,24,128]{3,2,1,0:T(8,128)(2,1)} %copy.62) | copy-start | bytes 9437188
  275.3 55.2 %copy-start.1 = (s32[48,64,16]{1,2,0:T(8,128)S(1)}, s32[48,64,16]{1,2,0:T(8,128)}, u32[]{:S(2)}) copy-start(s32[48,64,16]{1,2,0:T(8,128)} %param.8) | copy-start | bytes 589828
Sparse Core Ops, SparseCore 0:
  23.4 100.9 all-gather.2
  126.7 98.6 all-gather.4
where the time goes:
time: 339 us; the launch traced here: 337 us
  local copies, waits for them, and re-layouts  76.1 us (22%)
  blocking collectives  70.1 us (21%)
  matrix products  67.4 us (20%)
  other arithmetic  62 us (18%)
  waiting for transfers between devices  44.2 us (13%)
  between operations  13.5 us (4%)
  starting transfers between devices  4.01 us (1%)
    convert_element_type x1, other arithmetic, tile_update(): weights.astype(jnp.bfloat16)  50 us
    dot_general x1, matrix products, tile_update(): jnp.einsum('qhd,khd->hqk', query_heads, key_heads, preferred_element_type...  42.1 us
    all_gather x1, waiting for transfers between devices, local(): key_piece = lax.all_gather(key_mine, 'blk', axis=0, tiled=True)  41 us
    all_to_all x1, blocking collectives, local(): lax.all_to_all(outgoing, 'uly', split_axis=0, concat_axis=1, tiled=True)  41 us
    dot_general x1, matrix products, tile_update(): jnp.einsum('hqk,khd->hqd', weights.astype(jnp.bfloat16), value_heads, pre...  25.3 us
    all_gather x1, local copies, waits for them, and re-layouts, local(): key_piece = lax.all_gather(key_mine, 'blk', axis=0, tiled=True)  16.8 us
    all_gather x1, local copies, waits for them, and re-layouts, local(): lax.all_gather(value_mine, 'blk', axis=0, tiled=True)  16.6 us
    all_to_all x1, blocking collectives, local(): lax.all_to_all(key_local, 'uly', split_axis=1, concat_axis=0, tiled=True)  15.5 us
  transfers between devices with their start and end apart: 3, of which 2 were waited for; matrix products, arithmetic and copies ran while one was open for 44% of the time, Pallas kernels for 0%

commit v1 on v0

v1 whole, which is shorter than its diff:
```python
import functools
import math

import jax
import jax.numpy as jnp
from jax import lax
from jax.experimental import pallas as pl
from jax.experimental.pallas import tpu as pltpu
from jax.sharding import PartitionSpec as P

HEAD_DIM = 128
BLOCK = 128
NEGATIVE = -1e30
MESH = pl.DeviceIdType.MESH


def attend_kernel(
    blk_n, uly_n, group, q_any, k_any, v_any, bias_ref, o_any,
    qbuf, kbuf, vbuf, obuf,
    kv_send, k_recv, v_recv, q_send, q_recv, o_send, o_recv, local_sem,
):
    devices = blk_n * uly_n
    me = lax.axis_index("blk") * uly_n + lax.axis_index("uly")
    first = (me // group) * group
    place = me - first
    rows = q_any.shape[0]
    width = qbuf.shape[2]
    heads = width // HEAD_DIM
    keys_all = kbuf.shape[0] * kbuf.shape[1]
    qblocks = bias_ref.shape[1]
    scaling = 1.0 / math.sqrt(HEAD_DIM)

    def coords(device):
        return (device // uly_n, lax.rem(device, uly_n))

    def columns(position):
        return pl.ds(pl.multiple_of(position * width, HEAD_DIM), width)

    own = (
        pltpu.make_async_copy(k_any.at[:, columns(place)], kbuf.at[me], local_sem.at[0]),
        pltpu.make_async_copy(v_any.at[:, columns(place)], vbuf.at[me], local_sem.at[1]),
        pltpu.make_async_copy(q_any.at[:, columns(place)], qbuf.at[place], local_sem.at[2]),
    )
    for copy in own:
        copy.start()

    barrier = pltpu.get_barrier_semaphore()

    def greet(step, carry):
        other = lax.rem(me + step, devices)
        pl.semaphore_signal(barrier, inc=1, device_id=coords(other), device_id_type=MESH)
        return carry

    lax.fori_loop(1, devices, greet, 0)
    pl.semaphore_wait(barrier, devices - 1)

    def send_kv(step, carry):
        other = lax.rem(me + devices - step, devices)
        cols = columns(lax.rem(other, group))
        pltpu.make_async_remote_copy(
            src_ref=k_any.at[:, cols], dst_ref=kbuf.at[me],
            send_sem=kv_send.at[0], recv_sem=k_recv,
            device_id=coords(other), device_id_type=MESH,
        ).start()
        pltpu.make_async_remote_copy(
            src_ref=v_any.at[:, cols], dst_ref=vbuf.at[me],
            send_sem=kv_send.at[1], recv_sem=v_recv,
            device_id=coords(other), device_id_type=MESH,
        ).start()
        return carry

    lax.fori_loop(1, devices, send_kv, 0)

    def send_q(step, carry):
        there = lax.rem(place + group - step, group)
        pltpu.make_async_remote_copy(
            src_ref=q_any.at[:, columns(there)], dst_ref=qbuf.at[place],
            send_sem=q_send, recv_sem=q_recv.at[place],
            device_id=coords(first + there), device_id_type=MESH,
        ).start()
        return carry

    lax.fori_loop(1, group, send_q, 0)

    for copy in own:
        copy.wait()
    rest = pl.ds(0, devices - 1)
    pltpu.make_async_copy(kbuf.at[rest], kbuf.at[rest], k_recv).wait()
    pltpu.make_async_copy(vbuf.at[rest], vbuf.at[rest], v_recv).wait()

    def attend(source):
        for head in range(heads):
            cols = slice(head * HEAD_DIM, (head + 1) * HEAD_DIM)
            query = qbuf[source, :, cols]
            key = kbuf[:, :, cols].reshape(keys_all, HEAD_DIM)
            value = vbuf[:, :, cols].reshape(keys_all, HEAD_DIM)
            scores = lax.dot_general(
                query, key, (((1,), (1,)), ((), ())), preferred_element_type=jnp.float32
            )
            if rows >= BLOCK:
                count = rows // BLOCK
                parts = [
                    scores[b * BLOCK : (b + 1) * BLOCK]
                    + bias_ref[head, pl.ds(source * count + b, 1), :]
                    for b in range(count)
                ]
                scores = jnp.concatenate(parts, axis=0)
            else:
                scores = scores + bias_ref[head, pl.ds((source * rows) // BLOCK, 1), :]
            top = jnp.max(scores, axis=1, keepdims=True)
            weights = jnp.exp((scores - top) * scaling)
            total = jnp.sum(weights, axis=1, keepdims=True)
            mixed = jnp.dot(
                weights.astype(jnp.bfloat16), value, preferred_element_type=jnp.float32
            )
            obuf[source, :, cols] = (mixed / total).astype(jnp.bfloat16)

    attend(place)
    home = pltpu.make_async_copy(
        obuf.at[place], o_any.at[:, columns(place)], local_sem.at[3]
    )
    home.start()

    def visit(step, carry):
        source = lax.rem(place + step, group)
        pltpu.make_async_copy(qbuf.at[source], qbuf.at[source], q_recv.at[source]).wait()
        attend(source)
        pltpu.make_async_remote_copy(
            src_ref=obuf.at[source], dst_ref=o_any.at[:, columns(place)],
            send_sem=o_send, recv_sem=o_recv,
            device_id=coords(first + source), device_id_type=MESH,
        ).start()
        return carry

    lax.fori_loop(1, group, visit, 0)
    home.wait()
    pltpu.make_async_copy(kbuf.at[rest], kbuf.at[rest], kv_send.at[0]).wait()
    pltpu.make_async_copy(vbuf.at[rest], vbuf.at[rest], kv_send.at[1]).wait()
    peers = pl.ds(0, group - 1)
    pltpu.make_async_copy(qbuf.at[peers], qbuf.at[peers], q_send).wait()
    pltpu.make_async_copy(obuf.at[peers], obuf.at[peers], o_send).wait()
    pltpu.make_async_copy(obuf.at[peers], obuf.at[peers], o_recv).wait()


def local(blk_n, uly_n, queries, keys, values, block_lists, block_counts):
    heads_all, qblocks_all, listed = block_lists.shape
    share = math.gcd(blk_n, heads_all // uly_n)
    group = share * uly_n
    heads = heads_all // group
    groups = blk_n // share
    qblocks = qblocks_all // groups
    devices = blk_n * uly_n
    rows, key_rows = queries.shape[0], keys.shape[0]
    width = heads * HEAD_DIM
    keys_all = key_rows * devices

    me = lax.axis_index("blk") * uly_n + lax.axis_index("uly")
    place = lax.rem(me, group)
    lists = lax.dynamic_slice(
        block_lists, (place * heads, (me // group) * qblocks, 0), (heads, qblocks, listed)
    )
    counts = lax.dynamic_slice(
        block_counts, (place * heads, (me // group) * qblocks), (heads, qblocks)
    )
    usable = jnp.arange(listed, dtype=jnp.int32) < counts[:, :, None]
    chosen = jnp.where(usable, lists, -1)
    blocks = jnp.arange(keys_all // BLOCK, dtype=jnp.int32)
    member = jnp.any(chosen[:, :, :, None] == blocks, axis=2)
    bias = jnp.repeat(jnp.where(member, 0.0, NEGATIVE).astype(jnp.float32), BLOCK, axis=2)

    any_spec = pl.BlockSpec(memory_space=pl.ANY)
    dma = pltpu.SemaphoreType.DMA
    return pl.pallas_call(
        functools.partial(attend_kernel, blk_n, uly_n, group),
        out_shape=jax.ShapeDtypeStruct(queries.shape, queries.dtype),
        in_specs=[any_spec, any_spec, any_spec, pl.BlockSpec(memory_space=pltpu.VMEM)],
        out_specs=any_spec,
        scratch_shapes=[
            pltpu.VMEM((group, rows, width), jnp.bfloat16),
            pltpu.VMEM((devices, key_rows, width), jnp.bfloat16),
            pltpu.VMEM((devices, key_rows, width), jnp.bfloat16),
            pltpu.VMEM((group, rows, width), jnp.bfloat16),
            dma((2,)), dma, dma, dma, dma((group,)), dma, dma, dma((4,)),
        ],
        compiler_params=pltpu.CompilerParams(
            collective_id=0, has_side_effects=True, vmem_limit_bytes=60 * 1024 * 1024
        ),
    )(queries, keys, values, bias)


def solution(mesh):
    return jax.shard_map(
        functools.partial(local, mesh.shape["blk"], mesh.shape["uly"]),
        mesh=mesh,
        in_specs=(
            P(("blk", "uly"), None),
            P(("blk", "uly"), None),
            P(("blk", "uly"), None),
            P(),
            P(),
        ),
        out_specs=P(("blk", "uly"), None),
        check_vma=False,
    )
```

time: 339 us -> 154 us (0.45)
  the two profiles are of different devices: /device:TPU:0 before, /device:TPU:23 now
where the time goes in v1:
time: 154 us; the launch traced here: 153 us
  Pallas kernels  146 us (95%)
  local copies, waits for them, and re-layouts  6 us (4%)
    pallas_call x1, Pallas kernels, local(): pl.pallas_call(functools.partial(attend_kernel, blk_n, uly_n, group), out...  146 us
    unnamed x1, local copies, waits for them, and re-layouts  3.88 us

profile of v1, /device:TPU:23, one launch (start us, length us, event | category | flops | bytes accessed | tf_op | source)
XLA Modules:
  0.0 153.3 jit_solution(4901816225426937535)
XLA Ops:
  0.0 0.8 dynamic_slice.6
  0.8 0.8 dynamic-slice_select_fusion
  1.6 0.1 fusion
  1.7 0.1 copy.7
  1.7 0.3 broadcast_in_dim.22
  2.0 1.0 reshape.5.bias_ref
  3.0 146.4 %shard_map.55 = bf16[256,6144]{1,0:T(8,128)(2,1)} custom-call(bf16[256,6144]{1,0:T(8,128)(2,1)} %q_any.1, bf16[64,6144]{1,0:T(8,128)(2,1)} %k_any.1, bf16[64,6144]{1,0:T(8,128)(2,1)} %v_any.1, f32[3,32,2048]{2,1,0:T(8,128)} %reshape.5.bias_ref), custom_call_target="tpu_custom_call" | custom-call | tf_op jit(solution)/shard_map/pallas_call | solution.py:173
  149.5 3.9 %copy.9 = bf16[256,6144]{1,0:T(8,128)(2,1)} copy(bf16[256,6144]{1,0:T(8,128)(2,1)} %shard_map.55) | data formatting | bytes 6291456
  (1 shorter events, 0.0 us)

commit v2 on v1

--- a/solution.py
+++ b/solution.py
@@ -14,9 +14,19 @@
 MESH = pl.DeviceIdType.MESH
 
 
+def mix(a, b, n):
+    if n & (n - 1):
+        return lax.rem(n + b - a, n)
+    out, bit = 0, 1
+    while bit < n:
+        out = out + lax.rem(a // bit + b // bit, 2) * bit
+        bit *= 2
+    return out
+
+
 def attend_kernel(
     blk_n, uly_n, group, q_any, k_any, v_any, bias_ref, o_any,
-    qbuf, kbuf, vbuf, obuf,
+    qbuf, kbuf, vbuf, obuf, hot,
     kv_send, k_recv, v_recv, q_send, q_recv, o_send, o_recv, local_sem,
 ):
     devices = blk_n * uly_n
@@ -27,8 +37,8 @@
     width = qbuf.shape[2]
     heads = width // HEAD_DIM
     keys_all = kbuf.shape[0] * kbuf.shape[1]
-    qblocks = bias_ref.shape[1]
-    scaling = 1.0 / math.sqrt(HEAD_DIM)
+    flags = bias_ref.shape[2]
+    scaling = math.log2(math.e) / math.sqrt(HEAD_DIM)
 
     def coords(device):
         return (device // uly_n, lax.rem(device, uly_n))
@@ -55,7 +65,7 @@
     pl.semaphore_wait(barrier, devices - 1)
 
     def send_kv(step, carry):
-        other = lax.rem(me + devices - step, devices)
+        other = mix(me, step, devices)
         cols = columns(lax.rem(other, group))
         pltpu.make_async_remote_copy(
             src_ref=k_any.at[:, cols], dst_ref=kbuf.at[me],
@@ -72,7 +82,7 @@
     lax.fori_loop(1, devices, send_kv, 0)
 
     def send_q(step, carry):
-        there = lax.rem(place + group - step, group)
+        there = mix(place, step, group)
         pltpu.make_async_remote_copy(
             src_ref=q_any.at[:, columns(there)], dst_ref=qbuf.at[place],
             send_sem=q_send, recv_sem=q_recv.at[place],
@@ -81,6 +91,10 @@
         return carry
 
     lax.fori_loop(1, group, send_q, 0)
+
+    key_block = lax.broadcasted_iota(jnp.int32, hot.shape, 0) // BLOCK
+    lane = lax.broadcasted_iota(jnp.int32, hot.shape, 1)
+    hot[...] = jnp.where(key_block == lane, 1.0, 0.0).astype(jnp.bfloat16)
 
     for copy in own:
         copy.wait()
@@ -91,24 +105,24 @@
     def attend(source):
         for head in range(heads):
             cols = slice(head * HEAD_DIM, (head + 1) * HEAD_DIM)
-            query = qbuf[source, :, cols]
-            key = kbuf[:, :, cols].reshape(keys_all, HEAD_DIM)
+            spans = max(rows // BLOCK, 1)
+            flag = [
+                jnp.broadcast_to(
+                    bias_ref[head, pl.ds((source * rows) // BLOCK + b, 1), :],
+                    (rows // spans, flags),
+                ).astype(jnp.bfloat16)
+                for b in range(spans)
+            ]
+            query = jnp.concatenate([qbuf[source, :, cols], jnp.concatenate(flag, axis=0)], axis=1)
+            key = jnp.concatenate(
+                [kbuf[:, :, cols].reshape(keys_all, HEAD_DIM), hot[...]], axis=1
+            )
             value = vbuf[:, :, cols].reshape(keys_all, HEAD_DIM)
             scores = lax.dot_general(
                 query, key, (((1,), (1,)), ((), ())), preferred_element_type=jnp.float32
             )
-            if rows >= BLOCK:
-                count = rows // BLOCK
-                parts = [
-                    scores[b * BLOCK : (b + 1) * BLOCK]
-                    + bias_ref[head, pl.ds(source * count + b, 1), :]
-                    for b in range(count)
-                ]
-                scores = jnp.concatenate(parts, axis=0)
-            else:
-                scores = scores + bias_ref[head, pl.ds((source * rows) // BLOCK, 1), :]
             top = jnp.max(scores, axis=1, keepdims=True)
-            weights = jnp.exp((scores - top) * scaling)
+            weights = jnp.exp2((scores - top) * scaling)
             total = jnp.sum(weights, axis=1, keepdims=True)
             mixed = jnp.dot(
                 weights.astype(jnp.bfloat16), value, preferred_element_type=jnp.float32
@@ -122,7 +136,7 @@
     home.start()
 
     def visit(step, carry):
-        source = lax.rem(place + step, group)
+        source = mix(place, step, group)
         pltpu.make_async_copy(qbuf.at[source], qbuf.at[source], q_recv.at[source]).wait()
         attend(source)
         pltpu.make_async_remote_copy(
@@ -164,9 +178,11 @@
     )
     usable = jnp.arange(listed, dtype=jnp.int32) < counts[:, :, None]
     chosen = jnp.where(usable, lists, -1)
-    blocks = jnp.arange(keys_all // BLOCK, dtype=jnp.int32)
+    key_blocks = keys_all // BLOCK
+    flags = -(-key_blocks // HEAD_DIM) * HEAD_DIM
+    blocks = jnp.arange(flags, dtype=jnp.int32)
     member = jnp.any(chosen[:, :, :, None] == blocks, axis=2)
-    bias = jnp.repeat(jnp.where(member, 0.0, NEGATIVE).astype(jnp.float32), BLOCK, axis=2)
+    bias = jnp.where(member, 0.0, NEGATIVE).astype(jnp.float32)
 
     any_spec = pl.BlockSpec(memory_space=pl.ANY)
     dma = pltpu.SemaphoreType.DMA
@@ -180,6 +196,7 @@
             pltpu.VMEM((devices, key_rows, width), jnp.bfloat16),
             pltpu.VMEM((devices, key_rows, width), jnp.bfloat16),
             pltpu.VMEM((group, rows, width), jnp.bfloat16),
+            pltpu.VMEM((keys_all, flags), jnp.bfloat16),
             dma((2,)), dma, dma, dma, dma((group,)), dma, dma, dma((4,)),
         ],
         compiler_params=pltpu.CompilerParams(

time: 154 us -> 150 us (0.974)
  the two profiles are of different devices: /device:TPU:23 before, /device:TPU:0 now
where the time goes in v2:
time: 150 us
  Pallas kernels  143 us (95%)
  local copies, waits for them, and re-layouts  4.73 us (3%)
  other arithmetic  1.77 us (1%)
    pallas_call x1, Pallas kernels, local(): pl.pallas_call(functools.partial(attend_kernel, blk_n, uly_n, group), out...  143 us
    unnamed x1, local copies, waits for them, and re-layouts  3.88 us

profile of v2, /device:TPU:0, one launch (start us, length us, event | category | flops | bytes accessed | tf_op | source)
XLA Modules:
  0.0 149.7 jit_solution(10146968249802223300)
XLA Ops:
  0.0 0.8 dynamic_slice.6
  0.8 0.8 dynamic-slice_select_fusion
  1.6 0.1 copy.7
  1.7 0.3 fusion
  2.0 0.6 broadcast_select_fusion.bias_ref
  2.6 143.2 %shard_map.55 = bf16[256,6144]{1,0:T(8,128)(2,1)} custom-call(bf16[256,6144]{1,0:T(8,128)(2,1)} %q_any.1, bf16[64,6144]{1,0:T(8,128)(2,1)} %k_any.1, bf16[64,6144]{1,0:T(8,128)(2,1)} %v_any.1, f32[3,32,128]{2,1,0:T(8,128)} %broadcast_select_fusion.bias_ref), custom_call_target="tpu_custom_call" | custom-call | tf_op jit(solution)/shard_map/pallas_call | solution.py:189
  145.9 3.9 %copy.9 = bf16[256,6144]{1,0:T(8,128)(2,1)} copy(bf16[256,6144]{1,0:T(8,128)(2,1)} %shard_map.55) | data formatting | bytes 6291456
